TPU v7x, 128 devices: a whole 4x4x4 slice. The times are simulated.
128 devices in a mesh: seq: 8 (over z, core), row: 4 (over y), col: 4 (over x).
Axes of the slice: x: 4, y: 4, z: 4, core: 2. Of those that a mesh axis runs over, the one named last changes fastest.
Arguments:
- tokens: bfloat16 [4096, 4096], P('seq', ('row', 'col')), may hold values from -6 to 6
- lengths: int32 [16], replicated, may hold values from 1 to 1024, 4096 in all
- deal: int32 [16], replicated, may hold values from 0 to 15, each once
- pre_gain: float32 [4096], replicated, may hold values from 0.5 to 1.5
- w_inner: bfloat16 [4096, 2, 8192], P(None, None, ('row', 'col'))
- w_group: bfloat16 [4096, 2, 8, 128], P(None, None, 'row'), may hold values from -0.09375 to 0.09375
- w_step: bfloat16 [4096, 128], P(None, ('row', 'col')), may hold values from -0.09375 to 0.09375
- conv_inner: float32 [4, 8192], P(None, ('row', 'col')), may hold values from -0.5 to 0.5
- conv_group: float32 [4, 2, 8, 128], P(None, None, 'row'), may hold values from -0.5 to 0.5
- conv_bias_inner: float32 [8192], P(('row', 'col')), may hold values from -0.5 to 0.5
- conv_bias_group: float32 [2, 8, 128], P(None, 'row'), may hold values from -0.5 to 0.5
- edge_inner: bfloat16 [16, 3, 8192], P(None, None, ('row', 'col')), may hold values from -6 to 6
- edge_group: bfloat16 [16, 3, 2, 8, 128], P(None, None, None, 'row'), may hold values from -6 to 6
- init_states: float32 [16, 128, 64, 128], P(None, ('row', 'col')), may hold values from -1.25 to 1.25
- step_bias: float32 [128], P(('row', 'col')), may hold values from -5.3 to -2.3
- decay_log: float32 [128], P(('row', 'col')), may hold values from -3.9 to 0
- skip: float32 [128], P(('row', 'col')), may hold values from 0.5 to 1.5
- inner_gain: float32 [8192], P(('row', 'col')), may hold values from 0.5 to 1.5
- w_out: bfloat16 [8192, 4096], P(('row', 'col')), may hold values from -0.09375 to 0.09375
- final_gain: float32 [4096], replicated, may hold values from 0.5 to 1.5
- w_head: bfloat16 [4096, 32768], P(None, ('seq', 'row', 'col')), may hold values from -0.09375 to 0.09375
Outputs:
- hidden_out: bfloat16 [4096, 4096], P('seq', ('row', 'col'))
- final_states: float32 [16, 128, 64, 128], P('seq', ('row', 'col'))
- logits: float32 [16, 32768], P(None, ('seq', 'row', 'col'))
Inputs may be any that keep to these rules, and one draw needn't show every extreme that they name: The lengths sum to 4096 and the longest is exactly 1024. `deal`: each owner slot appears once.
All inputs are finite; a program needn't handle non-finite values.
Results may differ from a plain program's by a relative error of at most 0.012.
Values may be sent and summed in bfloat16 or wider, within the bound.
A program may use at most 128 MiB of HBM per device.

v0:
```python
import jax
import jax.numpy as jnp
from jax import lax
from jax.experimental import pallas as pl
from jax.experimental.pallas import tpu as pltpu
from jax.sharding import PartitionSpec as P

BLOCK = 256


EPSILON = 1e-05


MESH = pl.DeviceIdType.MESH
HALF = 256
FEAT = 256
VMEM_LIMIT = 62 * 1024 * 1024


def spot(axis, shift):
    size = lax.axis_size(axis)
    return lax.rem(lax.axis_index(axis) + shift + size, size)


def block_of(half, du, dv):
    row = spot("row", dv + half * (du - dv))
    col = spot("col", du + half * (dv - du))
    return row * lax.axis_size("col") + col


def remote(src, dst, sends, recvs, place, axis, shift):
    return pltpu.make_async_remote_copy(
        src_ref=src,
        dst_ref=dst,
        send_sem=sends.at[place],
        recv_sem=recvs.at[place],
        device_id={axis: spot(axis, shift)},
        device_id_type=MESH,
    )


def greet(peers):
    barrier = pltpu.get_barrier_semaphore()
    for peer in peers:
        pl.semaphore_signal(barrier, inc=1, device_id=peer, device_id_type=MESH)
    pl.semaphore_wait(barrier, len(peers))


PLANE = (("row", 1), ("row", -1), ("col", 1), ("col", -1))
AXES = (("col", "row"), ("row", "col"))
ORDER = (0, -1, 1, 2)
CHUNK = 64
PARTS = 4


def project_kernel(
    tokens,
    w_inner,
    w_group,
    w_step,
    gain,
    gate_out,
    chan_out,
    step_out,
    rim_out,
    raw_inner,
    raw_group,
    weights,
    wide_inner,
    wide_group,
    held,
    total,
    total_step,
    squares,
    load_sem,
    own_sem,
    sends,
    recvs,
    rim_stage,
    rim_land,
    rim_sems,
):
    depth = weights.shape[0]
    width = gate_out.shape[1]
    lanes = 128
    rows_part = depth // PARTS
    flat_inner = w_inner.reshape(2 * depth, width)
    flat_group = w_group.reshape(4 * depth, lanes)
    loads = []
    for part in range(PARTS):
        loads.append(
            (
                pltpu.make_async_copy(
                    flat_inner.at[pl.ds(2 * rows_part * part, 2 * rows_part)],
                    raw_inner.at[pl.ds(2 * rows_part * part, 2 * rows_part)],
                    load_sem.at[0, part],
                ),
                pltpu.make_async_copy(
                    flat_group.at[pl.ds(4 * rows_part * part, 4 * rows_part)],
                    raw_group.at[pl.ds(4 * rows_part * part, 4 * rows_part)],
                    load_sem.at[1, part],
                ),
            )
        )
    for part in range(PARTS):
        loads[part][0].start()
        loads[part][1].start()
    own = block_of(0, 0, 0)
    own_copy = pltpu.make_async_copy(tokens, held.at[own], own_sem)
    own_copy.start()
    greet([{axis: spot(axis, shift)} for axis, shift in PLANE + (("seq", 1), ("seq", -1))])
    messages = {}

    def send(half, number, du, dv, axis, shift, first, count, from_own=False):
        block = block_of(half, du, dv)
        rows = pl.ds(half * HALF + first, count)
        src = tokens.at[rows] if from_own else held.at[block, rows]
        copy = remote(
            src, held.at[block, rows], sends.at[half], recvs.at[half], number, axis, shift
        )
        copy.start()
        messages[half, number] = copy

    def arrive(half, *numbers):
        for number in numbers:
            messages[half, number].wait_recv()

    def spread(half, k, from_own=False):
        axis = AXES[half][1]
        send(half, 4 + 4 * k, ORDER[k], 0, axis, 1, 0, HALF, from_own)
        send(half, 5 + 4 * k, ORDER[k], 0, axis, -1, 0, HALF, from_own)

    def relay(half, k):
        axis = AXES[half][1]
        arrive(half, 4 + 4 * k)
        send(half, 6 + 4 * k, ORDER[k], -1, axis, 1, 0, HALF // 2)
        arrive(half, 5 + 4 * k)
        send(half, 7 + 4 * k, ORDER[k], 1, axis, -1, HALF // 2, HALF // 2)

    for half in (0, 1):
        axis = AXES[half][0]
        send(half, 0, 0, 0, axis, 1, 0, HALF, True)
        send(half, 1, 0, 0, axis, -1, 0, HALF, True)
    for half in (0, 1):
        spread(half, 0, True)
    group_local = lax.axis_index("col") * 2 // lax.axis_size("col")

    def untangle(part):
        loads[part][0].wait()
        loads[part][1].wait()

        def body(i, carry):
            base = pl.multiple_of(part * rows_part + i * CHUNK, CHUNK)
            for j in range(width // lanes):
                wide_inner[j] = raw_inner[
                    pl.ds(2 * base, 2 * CHUNK), j * lanes : (j + 1) * lanes
                ].astype(jnp.float32)
            wide_group[...] = raw_group[pl.ds(4 * base, 4 * CHUNK), :].astype(jnp.float32)
            for which in range(2):
                for j in range(width // lanes):
                    weights[
                        pl.ds(base, CHUNK), which * width + j * lanes : which * width + (j + 1) * lanes
                    ] = wide_inner[j, pl.ds(which, CHUNK, stride=2), :].astype(jnp.bfloat16)
                start = 2 * width + which * lanes
                weights[pl.ds(base, CHUNK), start : start + lanes] = wide_group[
                    pl.ds(2 * which + group_local, CHUNK, stride=4), :
                ].astype(jnp.bfloat16)
            return carry

        lax.fori_loop(0, rows_part // CHUNK, body, 0)

    total[...] = jnp.zeros_like(total)
    total_step[...] = jnp.zeros_like(total_step)
    squares[...] = jnp.zeros_like(squares)

    def multiply(half, du, dv):
        block = block_of(half, du, dv)
        rows = pl.ds(pl.multiple_of(half * HALF, HALF), HALF)
        column = pl.multiple_of(block * FEAT, FEAT)
        wide = held[block, rows, :].astype(jnp.float32)
        squares[rows, :] += wide[:, :lanes] * wide[:, :lanes] + wide[:, lanes:] * wide[:, lanes:]
        scaled = (wide * gain[:, pl.ds(column, FEAT)]).astype(jnp.bfloat16)
        total[rows, :] += jnp.dot(
            scaled, weights[pl.ds(column, FEAT), :], preferred_element_type=jnp.float32
        )
        total_step[rows, :] += lax.dot_general(
            scaled,
            w_step[:, pl.ds(column, FEAT)],
            (((1,), (1,)), ((), ())),
            preferred_element_type=jnp.float32,
        )

    def run(count, pick):
        def body(i, carry):
            half = lax.rem(i, 2)
            du, dv = pick(i // 2)
            multiply(half, du, dv)
            return carry

        lax.fori_loop(0, 2 * count, body, 0)

    untangle(0)
    for half in (0, 1):
        arrive(half, 0)
        send(half, 2, -1, 0, AXES[half][0], 1, 0, HALF // 2)
        spread(half, 1)
        arrive(half, 1)
        send(half, 3, 1, 0, AXES[half][0], -1, HALF // 2, HALF // 2)
        spread(half, 2)
    untangle(1)
    for half in (0, 1):
        relay(half, 0)
    untangle(2)
    for half in (0, 1):
        arrive(half, 2, 3)
        spread(half, 3)
    untangle(3)
    own_copy.wait()
    run(2, lambda j: (j, 0))
    for half in (0, 1):
        relay(half, 1)
    run(2, lambda j: (j + 2, 0))
    for half in (0, 1):
        relay(half, 2)
    run(4, lambda j: (-(j // 2), 2 * lax.rem(j, 2) - 1))
    for half in (0, 1):
        relay(half, 3)
    run(4, lambda j: (1 + j // 2, 2 * lax.rem(j, 2) - 1))
    for half in (0, 1):
        for k in range(4):
            arrive(half, 6 + 4 * k, 7 + 4 * k)
    run(4, lambda j: (j, 2))
    for half in (0, 1):
        for number in range(20):
            messages[half, number].wait_send()
    inv_rms = lax.rsqrt(jnp.sum(squares[...], axis=1, keepdims=True) / depth + EPSILON)
    last = total.shape[0] - rim_stage.shape[0]
    rim_stage[...] = (total[last:, width:] * inv_rms[last:]).astype(jnp.bfloat16)
    rim_copy = pltpu.make_async_remote_copy(
        src_ref=rim_stage,
        dst_ref=rim_land,
        send_sem=rim_sems.at[0],
        recv_sem=rim_sems.at[1],
        device_id={"seq": spot("seq", 1)},
        device_id_type=MESH,
    )
    rim_copy.start()
    gate_out[...] = (total[:, :width] * inv_rms).astype(jnp.bfloat16)
    chan_out[...] = (total[:, width:] * inv_rms).astype(jnp.bfloat16)
    step_out[...] = total_step[...] * inv_rms
    rim_copy.wait()
    rim_out[...] = rim_land[...]


def project(tokens, w_inner, w_group, w_step, pre_gain):
    rows, feat = tokens.shape
    depth, _, width = w_inner.shape
    heads = w_step.shape[1]
    state = w_group.shape[3]
    blocks = depth // feat
    columns = 2 * width + 2 * state
    vmem = pl.BlockSpec(memory_space=pltpu.VMEM)
    anywhere = pl.BlockSpec(memory_space=pl.ANY)
    return pl.pallas_call(
        project_kernel,
        out_shape=[
            jax.ShapeDtypeStruct((rows, width), jnp.bfloat16),
            jax.ShapeDtypeStruct((rows, width + 2 * state), jnp.bfloat16),
            jax.ShapeDtypeStruct((rows, heads), jnp.float32),
            jax.ShapeDtypeStruct((16, width + 2 * state), jnp.bfloat16),
        ],
        in_specs=[anywhere, anywhere, anywhere, vmem, vmem],
        out_specs=[vmem] * 4,
        scratch_shapes=[
            pltpu.VMEM((2 * depth, width), jnp.bfloat16),
            pltpu.VMEM((4 * depth, state), jnp.bfloat16),
            pltpu.VMEM((depth, columns), jnp.bfloat16),
            pltpu.VMEM((width // 128, 2 * CHUNK, 128), jnp.float32),
            pltpu.VMEM((4 * CHUNK, 128), jnp.float32),
            pltpu.VMEM((blocks, rows, feat), jnp.bfloat16),
            pltpu.VMEM((rows, columns), jnp.float32),
            pltpu.VMEM((rows, heads), jnp.float32),
            pltpu.VMEM((rows, 128), jnp.float32),
            pltpu.SemaphoreType.DMA((2, PARTS)),
            pltpu.SemaphoreType.DMA,
            pltpu.SemaphoreType.DMA((2, 20)),
            pltpu.SemaphoreType.DMA((2, 20)),
            pltpu.VMEM((16, width + 2 * state), jnp.bfloat16),
            pltpu.VMEM((16, width + 2 * state), jnp.bfloat16),
            pltpu.SemaphoreType.DMA((2,)),
        ],
        compiler_params=pltpu.CompilerParams(
            collective_id=0, has_side_effects=True, vmem_limit_bytes=VMEM_LIMIT
        ),
        name="project",
    )(tokens, w_inner, w_group, w_step.T, pre_gain[None, :])


NEVER = -1e30


def spans(lengths, deal):
    found = []
    begin = 0
    for k in range(lengths.shape[0]):
        end = begin + lengths[k]
        found.append((begin, end, deal[k]))
        begin = end
    return found


def head_column(values):
    heads = values.shape[0]
    places = lax.broadcasted_iota(jnp.int32, (heads, 1), 0)
    column = jnp.zeros((heads, 1), jnp.float32)
    for h in range(heads):
        column = jnp.where(places == h, values[h], column)
    return column


def by_head(tile, size):
    heads, width = tile.shape
    return jnp.reshape(
        jnp.broadcast_to(tile[:, None, :], (heads, size, width)), (heads * size, width)
    )


def columns_of(rows_by_head, count):
    heads = rows_by_head.shape[0]
    padding = jnp.zeros((128 - heads, count), jnp.float32)
    return jnp.concatenate([rows_by_head, padding], axis=0).T


def scan_kernel(
    lengths,
    deal,
    step_bias,
    decay_log,
    skip,
    chan,
    rim,
    step_raw,
    taps,
    bias,
    edges,
    init_states,
    partial_y,
    mixed,
    decay_column,
    decay_row,
    step_row,
    reach_column,
    carry_column,
    state_out,
    gain_out,
    finals_out,
    factor_out,
    longer,
    init,
    square,
    turned,
    states,
    factors,
    init_dot,
    load_sem,
):
    rows, width = chan.shape
    heads = step_raw.shape[1]
    requests = lengths.shape[0]
    inner = partial_y.shape[1]
    size = inner // heads
    state = (width - inner) // 2
    kernel = taps.shape[0]
    load = pltpu.make_async_copy(init_states, init, load_sem)
    load.start()
    first_row = lax.axis_index("seq") * rows
    places = spans(lengths, deal)

    def layout(shape, dim):
        local = lax.broadcasted_iota(jnp.int32, shape, dim)
        position = local + first_row
        start = jnp.zeros(shape, jnp.int32)
        owner = jnp.zeros(shape, jnp.int32)
        for begin, _, slot in places:
            started = position >= begin
            start = jnp.where(started, begin, start)
            owner = jnp.where(started, slot, owner)
        return local, position, position - start, owner

    local_c, position_c, offset_c, owner_c = layout((rows, 1), 0)
    local_r, _, offset_r, _ = layout((1, rows), 1)
    within_c = lax.rem(local_c, BLOCK)
    within_r = lax.rem(local_r, BLOCK)
    reach_c = jnp.minimum(offset_c, within_c)
    reach_r = jnp.minimum(offset_r, within_r)
    flag_c = offset_c > within_c
    flag_r = offset_r > within_r
    reach_column[...] = reach_c

    square[...] = jnp.zeros_like(square)
    square[:, :heads] = step_raw[...]
    raw_row = square[...].T[:heads] + head_column(step_bias)
    step = jnp.maximum(raw_row, 0.0) + jnp.log1p(jnp.exp(-jnp.abs(raw_row)))
    run = -jnp.exp(head_column(decay_log)) * step
    shift = 1
    while shift < BLOCK:
        run = run + jnp.where(reach_r >= shift, pltpu.roll(run, shift, 1), 0.0)
        shift *= 2
    run_c = columns_of(run, rows)
    step_row[...] = step
    decay_row[...] = run
    decay_column[...] = run_c
    coef_c = jnp.exp(run_c)
    carry_c = jnp.where(flag_c, coef_c, 0.0)
    init_c = jnp.where(flag_c, 0.0, coef_c)
    carry_column[0:BLOCK, :] = carry_c[0:BLOCK]
    carry_column[BLOCK:, :] = carry_c[BLOCK:] * carry_c[BLOCK - 1 : BLOCK, :]

    longer[0:8, :] = rim[8:16, :].astype(jnp.float32)
    longer[8:, :] = chan[...].astype(jnp.float32)
    summed = bias[...] + taps[kernel - 1 : kernel, :] * longer[8:, :]
    choices = lax.broadcasted_iota(jnp.int32, (rows, edges.shape[0]), 1)
    for back in range(1, kernel):
        slot = (kernel - 1 - back + offset_c) * requests + owner_c
        lookup = ((choices == slot) & (offset_c < back)).astype(jnp.float32).astype(jnp.bfloat16)
        from_edge = jnp.dot(lookup, edges[...], preferred_element_type=jnp.float32)
        value = jnp.where(offset_c >= back, longer[8 - back : 8 - back + rows, :], from_edge)
        summed = summed + taps[kernel - 1 - back : kernel - back, :] * value
    mixed[...] = (summed * (1.0 / (1.0 + jnp.exp(-summed)))).astype(jnp.bfloat16)
    turned[...] = mixed[:, :inner].astype(jnp.float32).T.astype(jnp.bfloat16)
    states[...] = jnp.zeros_like(states)
    factors[...] = jnp.zeros_like(factors)
    init_dot[...] = jnp.zeros_like(init_dot)
    load.wait()

    def pick(values, at):
        return jnp.sum(jnp.where(local_r == at, values, jnp.zeros_like(values)), axis=1, keepdims=True)

    def emit(at, index, slot):
        reach = pick(reach_r, at)
        flagged = pick(flag_r.astype(jnp.int32), at) > 0
        run_at = pick(run, at)
        keep = (local_r <= at) & (local_r >= at - reach)
        share = jnp.exp(jnp.where(keep, run_at - run, NEVER)) * step
        share = share.astype(jnp.bfloat16).astype(jnp.float32)
        spread = (turned[...].astype(jnp.float32) * by_head(share, size)).astype(jnp.bfloat16)
        value = jnp.dot(spread, mixed[:, inner : inner + state], preferred_element_type=jnp.float32)
        coef = jnp.exp(run_at)
        carry = jnp.broadcast_to(jnp.where(flagged, coef, 0.0), (heads, state))
        start = jnp.broadcast_to(jnp.where(flagged, 0.0, coef), (heads, state))
        late = at >= BLOCK
        first_gain = jnp.broadcast_to(
            jnp.where(pick(flag_r.astype(jnp.int32), BLOCK - 1) > 0, jnp.exp(pick(run, BLOCK - 1)), 0.0),
            (heads, state),
        )
        value = value + by_head(start, size) * init[slot]
        value = value + by_head(jnp.where(late, carry, 0.0), size) * states[0]
        states[index] = value
        factors[index] = carry * jnp.where(late, first_gain, 1.0)

    def request(k, begin):
        end = begin + lengths[k]
        slot = deal[k]
        low = begin - first_row
        high = end - first_row

        @pl.when((high > 0) & (low < rows))
        def _():
            chosen = (local_c >= low) & (local_c < high) & jnp.logical_not(flag_c)
            picked = jnp.where(chosen, mixed[:, inner + state :].astype(jnp.float32), 0.0)
            init_dot[...] += lax.dot_general(
                picked.astype(jnp.bfloat16),
                init[slot].astype(jnp.bfloat16),
                (((1,), (1,)), ((), ())),
                preferred_element_type=jnp.float32,
            )

            def place(j, carry):
                at = jnp.where(j < 2, BLOCK - 1 + j * BLOCK, high - 1)
                index = jnp.where(j < 2, j, 2 + slot)

                @pl.when((at >= low) & (at < high) & (at >= 0) & (at < rows))
                def _():
                    emit(at, index, slot)

                return carry

            lax.fori_loop(0, 3, place, 0)

        return end

    lax.fori_loop(0, requests, request, jnp.int32(0))
    state_out[...] = states[1].astype(jnp.bfloat16)
    gain_out[...] = factors[1]
    finals_out[...] = states[2:].astype(jnp.bfloat16)
    factor_out[...] = factors[2:]
    carried = lax.dot_general(
        mixed[BLOCK:, inner + state :],
        states[0].astype(jnp.bfloat16),
        (((1,), (1,)), ((), ())),
        preferred_element_type=jnp.float32,
    )
    for h in range(heads):
        span = slice(h * size, (h + 1) * size)
        value = skip[h] * mixed[:, span].astype(jnp.float32)
        value = value + init_c[:, h : h + 1] * init_dot[:, span]
        partial_y[0:BLOCK, span] = value[0:BLOCK]
        partial_y[BLOCK:, span] = value[BLOCK:] + carry_c[BLOCK:, h : h + 1] * carried[:, span]


def scan(
    lengths, deal, step_bias, decay_log, skip, chan, rim, step_raw, taps, bias, edges, init_states
):
    rows, width = chan.shape
    heads = step_raw.shape[1]
    requests, _, size, state = init_states.shape
    inner = heads * size
    smem = pl.BlockSpec(memory_space=pltpu.SMEM)
    vmem = pl.BlockSpec(memory_space=pltpu.VMEM)
    anywhere = pl.BlockSpec(memory_space=pl.ANY)
    f32, bf = jnp.float32, jnp.bfloat16
    shape = jax.ShapeDtypeStruct
    return pl.pallas_call(
        scan_kernel,
        out_shape=[
            shape((rows, inner), f32),
            shape((rows, width), bf),
            shape((rows, 128), f32),
            shape((heads, rows), f32),
            shape((heads, rows), f32),
            shape((rows, 1), jnp.int32),
            shape((rows, 128), f32),
            shape((inner, state), bf),
            shape((heads, state), f32),
            shape((requests, inner, state), bf),
            shape((requests, heads, state), f32),
        ],
        in_specs=[smem] * 5 + [vmem] * 6 + [anywhere],
        out_specs=[vmem] * 11,
        scratch_shapes=[
            pltpu.VMEM((rows + 8, width), f32),
            pltpu.VMEM((requests, inner, state), f32),
            pltpu.VMEM((rows, 128), f32),
            pltpu.VMEM((inner, rows), bf),
            pltpu.VMEM((requests + 2, inner, state), f32),
            pltpu.VMEM((requests + 2, heads, state), f32),
            pltpu.VMEM((rows, inner), f32),
            pltpu.SemaphoreType.DMA,
        ],
        compiler_params=pltpu.CompilerParams(vmem_limit_bytes=VMEM_LIMIT),
        name="scan",
    )(
        lengths,
        deal,
        step_bias,
        decay_log,
        skip,
        chan,
        rim,
        step_raw,
        taps,
        bias,
        edges,
        jnp.reshape(init_states, (requests, inner, state)),
    )


def slot_ends(lengths, deal, first_row, shape, dim):
    requests = lengths.shape[0]
    slots = lax.broadcasted_iota(jnp.int32, shape, dim)
    ends = jnp.zeros(shape, jnp.int32)
    end = -1 - first_row
    for k in range(requests):
        end = end + lengths[k]
        ends = jnp.where(slots == deal[k], end, ends)
    return ends


def finish_kernel(
    lengths,
    deal,
    partial_y,
    mixed,
    decay_column,
    decay_row,
    step_row,
    reach_column,
    carry_column,
    state_own,
    gain_own,
    finals_own,
    factor_own,
    gate_in,
    inner_gain,
    w_out,
    tokens,
    w_head,
    final_gain,
    hidden,
    final_states,
    logits,
    weights,
    head,
    partials,
    stage_far,
    stage_near,
    land_far,
    land_near,
    stage_far2,
    stage_near2,
    land_far2,
    land_near2,
    picks,
    rows_all,
    wide_rows,
    load_sem,
    sends,
    recvs,
    pick_sends,
    pick_recvs,
    row_sends,
    row_recvs,
    outputs,
    normed,
    scales,
    entry_held,
    land_state,
    land_gain,
    square_own,
    square_land,
    outbox,
    pair_land,
    pair_sum,
    final_land,
    far_sends,
    far_recvs,
):
    rows, feat = tokens.shape
    heads, inner = decay_row.shape[0], gate_in.shape[1]
    size = inner // heads
    state = state_own.shape[1]
    requests = lengths.shape[0]
    seq = lax.axis_size("seq")
    load_out = pltpu.make_async_copy(w_out, weights, load_sem.at[0])
    load_head = pltpu.make_async_copy(w_head, head, load_sem.at[1])
    load_out.start()
    load_head.start()
    plane = [(dr, dc) for dr in range(4) for dc in range(4) if dr or dc]
    peers = [{axis: spot(axis, shift)} for axis, shift in PLANE]
    peers += [{"seq": spot("seq", shift)} for shift in range(1, seq)]
    peers += [
        {"row": spot("row", dr), "col": spot("col", dc)}
        for dr, dc in plane
        if not ((dr == 0 and dc != 2) or (dc == 0 and dr != 2))
    ]
    greet(peers)
    extra = []

    def hand(src, dst, number, place):
        copy = pltpu.make_async_remote_copy(
            src_ref=src,
            dst_ref=dst,
            send_sem=far_sends.at[number],
            recv_sem=far_recvs.at[number],
            device_id=place,
            device_id_type=MESH,
        )
        copy.start()
        extra.append(copy)
        return copy

    hand(state_own, land_state.at[0], 0, {"seq": spot("seq", 1)})
    hand(gain_own, land_gain, 1, {"seq": spot("seq", 1)})
    hand(state_own, land_state.at[1], 2, {"seq": spot("seq", 2)})

    def inside(b, carry):
        place = pl.ds(pl.multiple_of(b * BLOCK, BLOCK), BLOCK)
        scores = lax.dot_general(
            mixed[place, inner + state :],
            mixed[place, inner : inner + state],
            (((1,), (1,)), ((), ())),
            preferred_element_type=jnp.float32,
        )
        target = lax.broadcasted_iota(jnp.int32, (BLOCK, BLOCK), 0)
        source = lax.broadcasted_iota(jnp.int32, (BLOCK, BLOCK), 1)
        keep = (source <= target) & (source >= target - reach_column[place, :])
        for h in range(heads):
            span = slice(h * size, (h + 1) * size)
            diff = decay_column[place, h : h + 1] - decay_row[h : h + 1, place]
            decay = jnp.exp(jnp.where(keep, diff, NEVER))
            weight = (scores * decay * step_row[h : h + 1, place]).astype(jnp.bfloat16)
            outputs[place, span] = partial_y[place, span] + jnp.dot(
                weight, mixed[place, span], preferred_element_type=jnp.float32
            )
        return carry

    lax.fori_loop(0, rows // BLOCK, inside, 0)
    for copy in extra:
        copy.wait_recv()
    entry = land_state[0].astype(jnp.float32) + by_head(land_gain[...], size) * land_state[
        1
    ].astype(jnp.float32)
    entry_held[...] = entry
    carried = lax.dot_general(
        mixed[:, inner + state :],
        entry.astype(jnp.bfloat16),
        (((1,), (1,)), ((), ())),
        preferred_element_type=jnp.float32,
    )
    squares = jnp.zeros((rows, 128), jnp.float32)
    left = lax.broadcasted_iota(jnp.int32, (rows, 128), 1) < size
    for tile in range(inner // 128):
        span = slice(tile * 128, (tile + 1) * 128)
        coef = jnp.where(
            left, carry_column[:, 2 * tile : 2 * tile + 1], carry_column[:, 2 * tile + 1 : 2 * tile + 2]
        )
        gate = gate_in[:, span].astype(jnp.float32)
        gated = (outputs[:, span] + coef * carried[:, span]) * (gate / (1.0 + jnp.exp(-gate)))
        squares = squares + gated * gated
        normed[:, span] = (gated * inner_gain[:, span]).astype(jnp.bfloat16)
    square_own[...] = jnp.broadcast_to(
        jnp.sum(squares.T, axis=0, keepdims=True), square_own.shape
    )
    partner = lax.axis_index("col") + 1 - 2 * lax.rem(lax.axis_index("col"), 2)
    square_copy = hand(square_own, square_land, 3, {"col": partner})
    load_out.wait()

    def compute(first, count, scale=None):
        def body(i, carry):
            half = lax.rem(i, 2)
            j = i // 2 + first
            dv = 2 - j // 4 - j // 8 + (j // 12) * 2
            du = 2 - lax.rem(j, 4) - lax.rem(j, 4) // 2 + (lax.rem(j, 4) // 3) * 2
            block = block_of(half, du, dv)
            place = pl.ds(pl.multiple_of(half * HALF, HALF), HALF)
            value = jnp.dot(
                normed[place, :],
                weights[:, pl.ds(pl.multiple_of(block * feat, feat), feat)],
                preferred_element_type=jnp.float32,
            )
            if scale is not None:
                value = value * scale[place, :]
            partials[half, j] = value
            return carry

        lax.fori_loop(0, 2 * count, body, 0)

    started = {}

    def send(half, number, src, dst, axis, shift):
        copy = remote(src, dst, sends.at[half], recvs.at[half], number, axis, shift)
        copy.start()
        started[half, number] = copy

    def far(half, values, stage, land, number, axis):
        for side in (0, 1):
            stage[side] = values[side * 128 : side * 128 + 128].astype(jnp.bfloat16)
            send(half, number + side, stage.at[side], land.at[side], axis, 1 - 2 * side)

    def near(half, side, values, far_land, far_number, stage, land, number, axis):
        started[half, far_number + side].wait_recv()
        extra = far_land[side].astype(jnp.float32)
        keep = slice(128 - 128 * side, 256 - 128 * side)
        mix = slice(128 * side, 128 * side + 128)
        stage[side, mix] = (values[mix] + extra).astype(jnp.bfloat16)
        stage[side, keep] = values[keep].astype(jnp.bfloat16)
        send(half, number + side, stage.at[side], land.at[side], axis, 1 - 2 * side)

    compute(0, 4)
    square_copy.wait_recv()
    both = square_own[0:1, :] + square_land[0:1, :]
    scale_row = lax.rsqrt(both / (2 * inner) + EPSILON)
    scale_tile = jnp.broadcast_to(scale_row, (128, rows)).T
    scales[...] = jnp.concatenate([scale_tile, scale_tile], axis=1)
    for k in range(4):
        for half in (0, 1):
            far(
                half,
                partials[half, k] * scales[half * HALF : half * HALF + HALF, :],
                stage_far.at[half, k],
                land_far.at[half, k],
                2 * k,
                AXES[half][1],
            )
    compute(4, 12, scales)
    core = lax.rem(lax.axis_index("seq"), 2)
    chip = lax.axis_index("seq") // 2
    chips = seq // 2

    def fill(o, carry):
        value = finals_own[o].astype(jnp.float32) + by_head(factor_own[o], size) * entry_held[...]
        outbox[lax.rem(o // 2, 2), o // 4, lax.rem(o, 2)] = value.astype(jnp.bfloat16)
        return carry

    lax.fori_loop(0, requests, fill, 0)
    pair_copy = hand(outbox.at[1 - core], pair_land, 4, {"seq": spot("seq", 1 - 2 * core)})
    for k in range(4):
        for half in (0, 1):
            for side in (0, 1):
                near(
                    half,
                    side,
                    partials[half, 4 + 4 * side + k],
                    land_far.at[half, k],
                    2 * k,
                    stage_near.at[half, k],
                    land_near.at[half, k],
                    8 + 2 * k,
                    AXES[half][1],
                )
    pair_copy.wait_recv()
    for d in range(chips):
        there = lax.rem(chip + d, chips)
        pair_sum[d] = (
            outbox[core, there].astype(jnp.float32) + pair_land[there].astype(jnp.float32)
        ).astype(jnp.bfloat16)
    final_copies = [
        hand(pair_sum.at[d], final_land.at[d - 1], 4 + d, {"seq": spot("seq", 2 * d)})
        for d in range(1, chips)
    ]
    for k in range(4):
        for half in (0, 1):
            axis = AXES[half][0]
            total = partials[half, 12 + k]
            for side in (0, 1):
                started[half, 8 + 2 * k + side].wait_recv()
                total = total + land_near[half, k, side].astype(jnp.float32)
            if k == 0:
                far(half, total, stage_far2.at[half], land_far2.at[half], 16, axis)
            elif k < 3:
                near(
                    half,
                    k - 1,
                    total,
                    land_far2.at[half],
                    16,
                    stage_near2.at[half],
                    land_near2.at[half],
                    18,
                    axis,
                )
            else:
                for side in (0, 1):
                    started[half, 18 + side].wait_recv()
                    total = total + land_near2[half, side].astype(jnp.float32)
                place = slice(half * HALF, half * HALF + HALF)
                hidden[place, :] = (tokens[place, :].astype(jnp.float32) + total).astype(
                    jnp.bfloat16
                )
    first_row = lax.axis_index("seq") * rows
    ends = slot_ends(lengths, deal, first_row, (requests, rows), 0)
    chooser = (ends == lax.broadcasted_iota(jnp.int32, (requests, rows), 1)).astype(jnp.bfloat16)
    picks[0] = jnp.dot(chooser, hidden[...], preferred_element_type=jnp.float32).astype(
        jnp.bfloat16
    )
    handed = []
    for shift in range(1, seq):
        copy = remote(
            picks.at[0], picks.at[shift], pick_sends, pick_recvs, shift, "seq", shift
        )
        copy.start()
        handed.append(copy)
    for copy in handed:
        copy.wait_recv()
    whole = picks[0].astype(jnp.float32)
    for shift in range(1, seq):
        whole = whole + picks[shift].astype(jnp.float32)
    own = block_of(0, 0, 0)
    rows_all[own] = whole.astype(jnp.bfloat16)
    for number, (dr, dc) in enumerate(plane):
        copy = pltpu.make_async_remote_copy(
            src_ref=rows_all.at[own],
            dst_ref=rows_all.at[own],
            send_sem=row_sends.at[number],
            recv_sem=row_recvs.at[number],
            device_id={"row": spot("row", dr), "col": spot("col", dc)},
            device_id_type=MESH,
        )
        copy.start()
        handed.append(copy)
    for copy in handed[seq - 1 :]:
        copy.wait_recv()
    for copy in final_copies:
        copy.wait_recv()
    final = pair_sum[0].astype(jnp.float32)
    for d in range(1, chips):
        final = final + final_land[d - 1].astype(jnp.float32)
    final_states[...] = final
    load_head.wait()
    total = jnp.zeros((requests, 128), jnp.float32)
    for block in range(len(plane) + 1):
        value = rows_all[block].astype(jnp.float32)
        wide_rows[:, block * feat : (block + 1) * feat] = value
        total = total + value[:, :128] * value[:, :128] + value[:, 128:] * value[:, 128:]
    depth = w_head.shape[0]
    scale = lax.rsqrt(jnp.sum(total, axis=1, keepdims=True) / depth + EPSILON)
    head_in = (wide_rows[...] * scale * final_gain[...]).astype(jnp.bfloat16)
    logits[...] = jnp.dot(head_in, head[...], preferred_element_type=jnp.float32)
    for copy in handed:
        copy.wait_send()
    for copy in list(started.values()) + extra:
        copy.wait_send()


def finish(lengths, deal, arrays, gate_in, inner_gain, w_out, tokens, w_head, final_gain):
    rows, feat = tokens.shape
    inner, depth = w_out.shape
    requests = lengths.shape[0]
    vocab = w_head.shape[1]
    seq = lax.axis_size("seq")
    state = arrays[7].shape[1]
    heads = arrays[8].shape[0]
    slots = requests // seq
    smem = pl.BlockSpec(memory_space=pltpu.SMEM)
    vmem = pl.BlockSpec(memory_space=pltpu.VMEM)
    anywhere = pl.BlockSpec(memory_space=pl.ANY)
    bf, f32 = jnp.bfloat16, jnp.float32
    return pl.pallas_call(
        finish_kernel,
        out_shape=[
            jax.ShapeDtypeStruct((rows, feat), bf),
            jax.ShapeDtypeStruct((slots, inner, state), f32),
            jax.ShapeDtypeStruct((requests, vocab), f32),
        ],
        in_specs=[smem, smem] + [vmem] * 13 + [anywhere, vmem, anywhere, vmem],
        out_specs=[vmem] * 3,
        scratch_shapes=[
            pltpu.VMEM((inner, depth), bf),
            pltpu.VMEM((depth, vocab), bf),
            pltpu.VMEM((2, 16, HALF, feat), f32),
            pltpu.VMEM((2, 4, 2, 128, feat), bf),
            pltpu.VMEM((2, 4, 2, 256, feat), bf),
            pltpu.VMEM((2, 4, 2, 128, feat), bf),
            pltpu.VMEM((2, 4, 2, 256, feat), bf),
            pltpu.VMEM((2, 2, 128, feat), bf),
            pltpu.VMEM((2, 2, 256, feat), bf),
            pltpu.VMEM((2, 2, 128, feat), bf),
            pltpu.VMEM((2, 2, 256, feat), bf),
            pltpu.VMEM((seq, requests, feat), bf),
            pltpu.VMEM((16, requests, feat), bf),
            pltpu.VMEM((requests, depth), f32),
            pltpu.SemaphoreType.DMA((2,)),
            pltpu.SemaphoreType.DMA((2, 20)),
            pltpu.SemaphoreType.DMA((2, 20)),
            pltpu.SemaphoreType.DMA((seq,)),
            pltpu.SemaphoreType.DMA((seq,)),
            pltpu.SemaphoreType.DMA((15,)),
            pltpu.SemaphoreType.DMA((15,)),
            pltpu.VMEM((rows, inner), f32),
            pltpu.VMEM((rows, inner), bf),
            pltpu.VMEM((rows, feat), f32),
            pltpu.VMEM((inner, state), f32),
            pltpu.VMEM((2, inner, state), bf),
            pltpu.VMEM((heads, state), f32),
            pltpu.VMEM((8, rows), f32),
            pltpu.VMEM((8, rows), f32),
            pltpu.VMEM((2, seq // 2, slots, inner, state), bf),
            pltpu.VMEM((seq // 2, slots, inner, state), bf),
            pltpu.VMEM((seq // 2, slots, inner, state), bf),
            pltpu.VMEM((seq // 2 - 1, slots, inner, state), bf),
            pltpu.SemaphoreType.DMA((8,)),
            pltpu.SemaphoreType.DMA((8,)),
        ],
        compiler_params=pltpu.CompilerParams(
            collective_id=1, has_side_effects=True, vmem_limit_bytes=VMEM_LIMIT
        ),
        name="finish",
    )(
        lengths,
        deal,
        *arrays,
        gate_in,
        inner_gain[None, :],
        w_out,
        tokens,
        w_head,
        final_gain[None, :],
    )


def per_device(
    tokens,
    lengths,
    deal,
    pre_gain,
    w_inner,
    w_group,
    w_step,
    conv_inner,
    conv_group,
    conv_bias_inner,
    conv_bias_group,
    edge_inner,
    edge_group,
    init_states,
    step_bias,
    decay_log,
    skip,
    inner_gain,
    w_out,
    final_gain,
    w_head,
):
    requests = lengths.shape[0]
    kernel, inner = conv_inner.shape
    state = w_group.shape[3]
    heads = w_step.shape[1]
    local = lax.axis_index("col") * w_group.shape[2] // lax.axis_size("col")

    def pick_group(table, axis):
        return lax.dynamic_index_in_dim(table, local, axis, keepdims=False)

    taps = jnp.concatenate(
        [conv_inner, jnp.reshape(pick_group(conv_group, 2), (kernel, 2 * state))], axis=1
    )
    bias = jnp.concatenate(
        [conv_bias_inner, jnp.reshape(pick_group(conv_bias_group, 1), (2 * state,))]
    )[None, :]
    edges = jnp.concatenate(
        [
            jnp.transpose(edge_inner, (1, 0, 2)),
            jnp.transpose(
                jnp.reshape(pick_group(edge_group, 3), (requests, kernel - 1, 2 * state)), (1, 0, 2)
            ),
        ],
        axis=2,
    )
    edges = jnp.reshape(edges, ((kernel - 1) * requests, inner + 2 * state))
    gate_in, chan, step_raw, rim = project(tokens, w_inner, w_group, w_step, pre_gain)
    arrays = scan(
        lengths, deal, step_bias, decay_log, skip, chan, rim, step_raw, taps, bias, edges, init_states
    )
    hidden_out, final_states, logits = finish(
        lengths, deal, arrays, gate_in, inner_gain, w_out, tokens, w_head, final_gain
    )
    final_states = jnp.reshape(
        final_states, (final_states.shape[0], heads, inner // heads, state)
    )
    return (hidden_out, final_states, logits)


def solution(mesh):
    in_specs = (
        P("seq", ("row", "col")),
        P(),
        P(),
        P(),
        P(None, None, ("row", "col")),
        P(None, None, "row", None),
        P(None, ("row", "col")),
        P(None, ("row", "col")),
        P(None, None, "row", None),
        P(("row", "col")),
        P(None, "row", None),
        P(None, None, ("row", "col")),
        P(None, None, None, "row", None),
        P(None, ("row", "col"), None, None),
        P(("row", "col")),
        P(("row", "col")),
        P(("row", "col")),
        P(("row", "col")),
        P(("row", "col"), None),
        P(),
        P(None, ("seq", "row", "col")),
    )
    out_specs = (
        P("seq", ("row", "col")),
        P("seq", ("row", "col"), None, None),
        P(None, ("seq", "row", "col")),
    )
    return jax.shard_map(
        per_device, mesh=mesh, in_specs=in_specs, out_specs=out_specs, check_vma=False
    )
```

profile of v0, /device:TPU:0, one launch (start us, length us, event | category | flops | bytes accessed | tf_op | source)
XLA Modules:
  0.0 116.2 jit_solution(2220828543110658114)
XLA Ops:
  0.6 0.0 copy-start
  0.7 0.7 constant_dynamic-slice_fusion.1
  1.4 0.7 pad_maximum_fusion.2
  2.0 0.6 broadcast_in_dim.13.bias
  2.6 0.7 dynamic-slice_reduce_fusion
  3.4 1.3 %pad_maximum_fusion.1.taps = f32[4,768]{1,0:T(4,128)} fusion(f32[4,256]{1,0:T(4,128)S(1)} %bitcast.25, f32[4,512]{1,0:T(4,128)} %param.28), kind=kLoop, calls=%fused_computation.1 | loop fusion | flops 3072 | bytes 24576 | tf_op jit(solution)/shard_map/concatenate | solution.py:1013
  4.7 0.0 copy-done
  4.7 0.1 constant_dynamic-slice_fusion
  4.8 1.4 %pad_maximum_fusion = bf16[3,16,768]{2,1,0:T(8,128)(2,1)} fusion(bf16[3,16,256]{2,1,0:T(8,128)(2,1)S(1)} %bitcast.19, bf16[3,16,512]{2,1,0:T(8,128)(2,1)} %bitcast.21), kind=kLoop, calls=%fused_computation | loop fusion | flops 147456 | bytes 147456 | tf_op jit(solution)/shard_map/concatenate | solution.py:1019
  6.2 40.0 %project.1 = (bf16[512,512]{1,0:T(8,128)(2,1)}, bf16[512,768]{1,0:T(8,128)(2,1)}, f32[512,8]{1,0:T(8,128)}, bf16[16,768]{1,0:T(8,128)(2,1)}) custom-call(bf16[512,256]{1,0:T(8,128)(2,1)} %tokens.3, bf16[4096,2,512]{2,1,0:T(2,128)(2,1)} %w_inner.1, bf16[4096,2,2,128]{3,2,1,0:T(2,128)(2,1)} %w_group.1, bf16[8,4096]{1,0:T(8,128)(2,1)} %bitcast.20, ...), custom_call_target="tpu_custom_call" | custom-call | tf_op jit(solution)/shard_map/project/pallas_call | solution.py:264
  46.3 9.8 %scan.1 = (f32[512,512]{1,0:T(8,128)}, bf16[512,768]{1,0:T(8,128)(2,1)}, f32[512,128]{1,0:T(8,128)}, f32[8,512]{1,0:T(8,128)}, f32[8,512]{1,0:T(8,128)}, /*index...) custom-call(s32[16]{0:T(128)} %lengths.3, ...), custom_call_target="tpu_custom_call" | custom-call | tf_op jit(solution)/shard_map/scan/pallas_call | solution.py:523
  56.0 55.3 %finish.1 = (bf16[512,256]{1,0:T(8,128)(2,1)}, f32[2,512,128]{2,1,0:T(8,128)}, f32[16,256]{1,0:T(8,128)}) custom-call(s32[16]{0:T(128)} %lengths.3, s32[16]{0:T(128)} %deal.3, f32[512,512]{1,0:T(8,128)} %get-tuple-element.24.partial_y, bf16[512,768]{1,0:T(8,128)(2,1)} %get-tuple-element.25.mixed, f32[512,128]{1,0:T(8,128)} %get-tuple-element.26.decay_column, ...), custom_call_target="tpu_custom_call" | custom-call | tf_op jit(solution)/shard_map/finish/pallas_call | solution.py:918
  111.3 1.7 %copy.31 = bf16[512,256]{1,0:T(8,128)(2,1)} copy(bf16[512,256]{1,0:T(8,128)(2,1)} %get-tuple-element.42) | data formatting | bytes 524288
  113.0 1.9 %copy.32 = f32[2,8,64,128]{3,2,1,0:T(8,128)} copy(f32[2,8,64,128]{3,2,1,0:T(8,128)} %bitcast.17) | data formatting | bytes 1048576
  114.9 1.3 %copy.33 = f32[16,256]{1,0:T(8,128)} copy(f32[16,256]{1,0:T(8,128)} %get-tuple-element.44) | data formatting | bytes 32768
  (3 shorter events, 0.0 us)
Async XLA Ops:
  0.6 4.0 %copy-start = (bf16[16,3,2,2,128]{4,3,2,1,0:T(2,128)(2,1)S(1)}, bf16[16,3,2,2,128]{4,3,2,1,0:T(2,128)(2,1)}, u32[]{:S(2)}) copy-start(bf16[16,3,2,2,128]{4,3,2,1,0:T(2,128)(2,1)} %param.33) | copy-start | bytes 147460
where the time goes:
time: 117 us; the launch traced here: 116 us
  Pallas kernels  105 us (90%)
  local copies, waits for them, and re-layouts  7 us (6%)
  other arithmetic  3.42 us (3%)
    pallas_call x1, Pallas kernels, finish(): pl.pallas_call(finish_kernel, out_shape=[jax.ShapeDtypeStruct((rows, feat...  55.3 us
    pallas_call x1, Pallas kernels, project(): pl.pallas_call(project_kernel, out_shape=[jax.ShapeDtypeStruct((rows, wid...  40 us
    pallas_call x1, Pallas kernels, scan(): pl.pallas_call(scan_kernel, out_shape=[shape((rows, inner), f32), shape((...  9.76 us
    unnamed x6, local copies, waits for them, and re-layouts  4.89 us

commit v1 on v0

--- a/solution.py
+++ b/solution.py
@@ -226,10 +226,10 @@
     for half in (0, 1):
         relay(half, 3)
     run(4, lambda j: (1 + j // 2, 2 * lax.rem(j, 2) - 1))
-    for half in (0, 1):
-        for k in range(4):
+    for k in range(4):
+        for half in (0, 1):
             arrive(half, 6 + 4 * k, 7 + 4 * k)
-    run(4, lambda j: (j, 2))
+        run(1, lambda j: (ORDER[k], 2))
     for half in (0, 1):
         for number in range(20):
             messages[half, number].wait_send()
@@ -340,9 +340,12 @@
     chan,
     rim,
     step_raw,
-    taps,
-    bias,
-    edges,
+    conv_inner,
+    conv_group,
+    bias_inner,
+    bias_group,
+    edge_inner,
+    edge_group,
     init_states,
     partial_y,
     mixed,
@@ -362,6 +365,8 @@
     states,
     factors,
     init_dot,
+    taps,
+    edges,
     load_sem,
 ):
     rows, width = chan.shape
@@ -370,7 +375,7 @@
     inner = partial_y.shape[1]
     size = inner // heads
     state = (width - inner) // 2
-    kernel = taps.shape[0]
+    kernel = conv_inner.shape[0]
     load = pltpu.make_async_copy(init_states, init, load_sem)
     load.start()
     first_row = lax.axis_index("seq") * rows
@@ -416,6 +421,24 @@
     carry_column[0:BLOCK, :] = carry_c[0:BLOCK]
     carry_column[BLOCK:, :] = carry_c[BLOCK:] * carry_c[BLOCK - 1 : BLOCK, :]
 
+    second = lax.axis_index("col") * 2 // lax.axis_size("col") > 0
+    bias = taps.at[kernel : kernel + 1]
+    taps[0:kernel, :inner] = conv_inner[...]
+    bias[:, :inner] = bias_inner[...]
+    for back in range(kernel - 1):
+        edges[back * requests : (back + 1) * requests, :inner] = edge_inner[back]
+    for which in range(2):
+        span = slice(inner + which * state, inner + (which + 1) * state)
+        for tap in range(kernel):
+            pair = conv_group[tap, which]
+            taps[tap : tap + 1, span] = jnp.where(second, pair[1:2], pair[0:1])
+        pair = bias_group[which]
+        bias[:, span] = jnp.where(second, pair[1:2], pair[0:1])
+        for back in range(kernel - 1):
+            pairs = edge_group[:, back, which].astype(jnp.float32)
+            edges[back * requests : (back + 1) * requests, span] = jnp.where(
+                second, pairs[:, 1, :], pairs[:, 0, :]
+            ).astype(jnp.bfloat16)
     longer[0:8, :] = rim[8:16, :].astype(jnp.float32)
     longer[8:, :] = chan[...].astype(jnp.float32)
     summed = bias[...] + taps[kernel - 1 : kernel, :] * longer[8:, :]
@@ -509,7 +532,21 @@
 
 
 def scan(
-    lengths, deal, step_bias, decay_log, skip, chan, rim, step_raw, taps, bias, edges, init_states
+    lengths,
+    deal,
+    step_bias,
+    decay_log,
+    skip,
+    chan,
+    rim,
+    step_raw,
+    conv_inner,
+    conv_group,
+    bias_inner,
+    bias_group,
+    edge_inner,
+    edge_group,
+    init_states,
 ):
     rows, width = chan.shape
     heads = step_raw.shape[1]
@@ -535,7 +572,7 @@
             shape((requests, inner, state), bf),
             shape((requests, heads, state), f32),
         ],
-        in_specs=[smem] * 5 + [vmem] * 6 + [anywhere],
+        in_specs=[smem] * 5 + [vmem] * 9 + [anywhere],
         out_specs=[vmem] * 11,
         scratch_shapes=[
             pltpu.VMEM((rows + 8, width), f32),
@@ -545,6 +582,8 @@
             pltpu.VMEM((requests + 2, inner, state), f32),
             pltpu.VMEM((requests + 2, heads, state), f32),
             pltpu.VMEM((rows, inner), f32),
+            pltpu.VMEM((8, width), f32),
+            pltpu.VMEM(((conv_inner.shape[0] - 1) * requests, width), bf),
             pltpu.SemaphoreType.DMA,
         ],
         compiler_params=pltpu.CompilerParams(vmem_limit_bytes=VMEM_LIMIT),
@@ -558,11 +597,18 @@
         chan,
         rim,
         step_raw,
-        taps,
-        bias,
-        edges,
+        conv_inner,
+        conv_group,
+        bias_inner[None, :],
+        bias_group,
+        jnp.transpose(edge_inner, (1, 0, 2)),
+        edge_group,
         jnp.reshape(init_states, (requests, inner, state)),
     )
+
+
+PICKS = 16
+PITCH = HALF + PICKS
 
 
 def slot_ends(lengths, deal, first_row, shape, dim):
@@ -634,6 +680,10 @@
     final_land,
     far_sends,
     far_recvs,
+    row_stage,
+    row_land,
+    early_sends,
+    early_recvs,
 ):
     rows, feat = tokens.shape
     heads, inner = decay_row.shape[0], gate_in.shape[1]
@@ -717,12 +767,23 @@
         gate = gate_in[:, span].astype(jnp.float32)
         gated = (outputs[:, span] + coef * carried[:, span]) * (gate / (1.0 + jnp.exp(-gate)))
         squares = squares + gated * gated
-        normed[:, span] = (gated * inner_gain[:, span]).astype(jnp.bfloat16)
+        value = (gated * inner_gain[:, span]).astype(jnp.bfloat16)
+        normed[0:HALF, span] = value[0:HALF]
+        normed[PITCH : PITCH + HALF, span] = value[HALF:]
     square_own[...] = jnp.broadcast_to(
         jnp.sum(squares.T, axis=0, keepdims=True), square_own.shape
     )
     partner = lax.axis_index("col") + 1 - 2 * lax.rem(lax.axis_index("col"), 2)
     square_copy = hand(square_own, square_land, 3, {"col": partner})
+    ends = slot_ends(lengths, deal, lax.axis_index("seq") * rows, (requests, rows), 0)
+    chosen = ends == lax.broadcasted_iota(jnp.int32, (requests, rows), 1)
+    chooser = chosen.astype(jnp.float32).astype(jnp.bfloat16)
+    picked = jnp.dot(chooser[:, :HALF], normed[0:HALF, :], preferred_element_type=jnp.float32)
+    picked = picked + jnp.dot(
+        chooser[:, HALF:], normed[PITCH : PITCH + HALF, :], preferred_element_type=jnp.float32
+    )
+    for half in (0, 1):
+        normed[half * PITCH + HALF : half * PITCH + PITCH, :] = picked.astype(jnp.bfloat16)
     load_out.wait()
 
     def compute(first, count, scale=None):
@@ -732,7 +793,7 @@
             dv = 2 - j // 4 - j // 8 + (j // 12) * 2
             du = 2 - lax.rem(j, 4) - lax.rem(j, 4) // 2 + (lax.rem(j, 4) // 3) * 2
             block = block_of(half, du, dv)
-            place = pl.ds(pl.multiple_of(half * HALF, HALF), HALF)
+            place = pl.ds(pl.multiple_of(half * PITCH, PICKS), PITCH)
             value = jnp.dot(
                 normed[place, :],
                 weights[:, pl.ds(pl.multiple_of(block * feat, feat), feat)],
@@ -771,18 +832,42 @@
     both = square_own[0:1, :] + square_land[0:1, :]
     scale_row = lax.rsqrt(both / (2 * inner) + EPSILON)
     scale_tile = jnp.broadcast_to(scale_row, (128, rows)).T
-    scales[...] = jnp.concatenate([scale_tile, scale_tile], axis=1)
+    wide_scale = jnp.concatenate([scale_tile, scale_tile], axis=1)
+    pick_scale = jnp.broadcast_to(
+        jnp.sum(jnp.where(chosen, scale_row, 0.0), axis=1, keepdims=True), (requests, feat)
+    )
+    for half in (0, 1):
+        start = half * PITCH
+        scales[start : start + HALF, :] = wide_scale[half * HALF : half * HALF + HALF]
+        scales[start + HALF : start + PITCH, :] = pick_scale
     for k in range(4):
         for half in (0, 1):
             far(
                 half,
-                partials[half, k] * scales[half * HALF : half * HALF + HALF, :],
+                partials[half, k, 0:HALF] * scales[half * PITCH : half * PITCH + HALF, :],
                 stage_far.at[half, k],
                 land_far.at[half, k],
                 2 * k,
                 AXES[half][1],
             )
     compute(4, 12, scales)
+    row_copies = []
+    for j in range(15):
+        dv, du = (2, 1, -1, 0)[j // 4], (2, 1, -1, 0)[j % 4]
+        value = partials[0, j, HALF:PITCH]
+        if j < 4:
+            value = value * pick_scale
+        row_stage[j] = value.astype(jnp.bfloat16)
+        copy = pltpu.make_async_remote_copy(
+            src_ref=row_stage.at[j],
+            dst_ref=row_land.at[j],
+            send_sem=early_sends.at[j],
+            recv_sem=early_recvs.at[j],
+            device_id={"row": spot("row", dv), "col": spot("col", du)},
+            device_id_type=MESH,
+        )
+        copy.start()
+        row_copies.append(copy)
     core = lax.rem(lax.axis_index("seq"), 2)
     chip = lax.axis_index("seq") // 2
     chips = seq // 2
@@ -800,7 +885,7 @@
                 near(
                     half,
                     side,
-                    partials[half, 4 + 4 * side + k],
+                    partials[half, 4 + 4 * side + k, 0:HALF],
                     land_far.at[half, k],
                     2 * k,
                     stage_near.at[half, k],
@@ -808,6 +893,40 @@
                     8 + 2 * k,
                     AXES[half][1],
                 )
+    row_total = partials[0, 15, HALF:PITCH]
+    row_total = row_total + jnp.dot(chooser, tokens[...], preferred_element_type=jnp.float32)
+    for j, copy in enumerate(row_copies):
+        copy.wait_recv()
+        row_total = row_total + row_land[j].astype(jnp.float32)
+    picks[0] = row_total.astype(jnp.bfloat16)
+    handed = []
+    for shift in range(1, seq):
+        copy = remote(
+            picks.at[0], picks.at[shift], pick_sends, pick_recvs, shift, "seq", shift
+        )
+        copy.start()
+        handed.append(copy)
+    own = block_of(0, 0, 0)
+
+    def gather_rows():
+        for copy in handed[: seq - 1]:
+            copy.wait_recv()
+        whole = picks[0].astype(jnp.float32)
+        for shift in range(1, seq):
+            whole = whole + picks[shift].astype(jnp.float32)
+        rows_all[own] = whole.astype(jnp.bfloat16)
+        for number, (dr, dc) in enumerate(plane):
+            copy = pltpu.make_async_remote_copy(
+                src_ref=rows_all.at[own],
+                dst_ref=rows_all.at[own],
+                send_sem=row_sends.at[number],
+                recv_sem=row_recvs.at[number],
+                device_id={"row": spot("row", dr), "col": spot("col", dc)},
+                device_id_type=MESH,
+            )
+            copy.start()
+            handed.append(copy)
+
     pair_copy.wait_recv()
     for d in range(chips):
         there = lax.rem(chip + d, chips)
@@ -819,9 +938,11 @@
         for d in range(1, chips)
     ]
     for k in range(4):
+        if k == 2:
+            gather_rows()
         for half in (0, 1):
             axis = AXES[half][0]
-            total = partials[half, 12 + k]
+            total = partials[half, 12 + k, 0:HALF]
             for side in (0, 1):
                 started[half, 8 + 2 * k + side].wait_recv()
                 total = total + land_near[half, k, side].astype(jnp.float32)
@@ -847,37 +968,6 @@
                 hidden[place, :] = (tokens[place, :].astype(jnp.float32) + total).astype(
                     jnp.bfloat16
                 )
-    first_row = lax.axis_index("seq") * rows
-    ends = slot_ends(lengths, deal, first_row, (requests, rows), 0)
-    chooser = (ends == lax.broadcasted_iota(jnp.int32, (requests, rows), 1)).astype(jnp.bfloat16)
-    picks[0] = jnp.dot(chooser, hidden[...], preferred_element_type=jnp.float32).astype(
-        jnp.bfloat16
-    )
-    handed = []
-    for shift in range(1, seq):
-        copy = remote(
-            picks.at[0], picks.at[shift], pick_sends, pick_recvs, shift, "seq", shift
-        )
-        copy.start()
-        handed.append(copy)
-    for copy in handed:
-        copy.wait_recv()
-    whole = picks[0].astype(jnp.float32)
-    for shift in range(1, seq):
-        whole = whole + picks[shift].astype(jnp.float32)
-    own = block_of(0, 0, 0)
-    rows_all[own] = whole.astype(jnp.bfloat16)
-    for number, (dr, dc) in enumerate(plane):
-        copy = pltpu.make_async_remote_copy(
-            src_ref=rows_all.at[own],
-            dst_ref=rows_all.at[own],
-            send_sem=row_sends.at[number],
-            recv_sem=row_recvs.at[number],
-            device_id={"row": spot("row", dr), "col": spot("col", dc)},
-            device_id_type=MESH,
-        )
-        copy.start()
-        handed.append(copy)
     for copy in handed[seq - 1 :]:
         copy.wait_recv()
     for copy in final_copies:
@@ -898,7 +988,7 @@
     logits[...] = jnp.dot(head_in, head[...], preferred_element_type=jnp.float32)
     for copy in handed:
         copy.wait_send()
-    for copy in list(started.values()) + extra:
+    for copy in list(started.values()) + extra + row_copies:
         copy.wait_send()
 
 
@@ -927,7 +1017,7 @@
         scratch_shapes=[
             pltpu.VMEM((inner, depth), bf),
             pltpu.VMEM((depth, vocab), bf),
-            pltpu.VMEM((2, 16, HALF, feat), f32),
+            pltpu.VMEM((2, 16, PITCH, feat), f32),
             pltpu.VMEM((2, 4, 2, 128, feat), bf),
             pltpu.VMEM((2, 4, 2, 256, feat), bf),
             pltpu.VMEM((2, 4, 2, 128, feat), bf),
@@ -947,8 +1037,8 @@
             pltpu.SemaphoreType.DMA((15,)),
             pltpu.SemaphoreType.DMA((15,)),
             pltpu.VMEM((rows, inner), f32),
-            pltpu.VMEM((rows, inner), bf),
-            pltpu.VMEM((rows, feat), f32),
+            pltpu.VMEM((2 * PITCH, inner), bf),
+            pltpu.VMEM((2 * PITCH, feat), f32),
             pltpu.VMEM((inner, state), f32),
             pltpu.VMEM((2, inner, state), bf),
             pltpu.VMEM((heads, state), f32),
@@ -960,6 +1050,10 @@
             pltpu.VMEM((seq // 2 - 1, slots, inner, state), bf),
             pltpu.SemaphoreType.DMA((8,)),
             pltpu.SemaphoreType.DMA((8,)),
+            pltpu.VMEM((15, requests, feat), bf),
+            pltpu.VMEM((15, requests, feat), bf),
+            pltpu.SemaphoreType.DMA((15,)),
+            pltpu.SemaphoreType.DMA((15,)),
         ],
         compiler_params=pltpu.CompilerParams(
             collective_id=1, has_side_effects=True, vmem_limit_bytes=VMEM_LIMIT
@@ -976,6 +1070,29 @@
         w_head,
         final_gain[None, :],
     )
+
+
+def deliver_kernel(*refs):
+    count = len(refs) // 2
+    sems = refs[-1]
+    copies = [
+        pltpu.make_async_copy(refs[i], refs[count + i], sems.at[i]) for i in range(count)
+    ]
+    for copy in copies:
+        copy.start()
+    for copy in copies:
+        copy.wait()
+
+
+def deliver(*arrays):
+    return pl.pallas_call(
+        deliver_kernel,
+        out_shape=[jax.ShapeDtypeStruct(a.shape, a.dtype) for a in arrays],
+        in_specs=[pl.BlockSpec(memory_space=pltpu.VMEM)] * len(arrays),
+        out_specs=[pl.BlockSpec(memory_space=pl.ANY)] * len(arrays),
+        scratch_shapes=[pltpu.SemaphoreType.DMA((len(arrays),))],
+        name="deliver",
+    )(*arrays)
 
 
 def per_device(
@@ -1001,38 +1118,31 @@
     final_gain,
     w_head,
 ):
-    requests = lengths.shape[0]
-    kernel, inner = conv_inner.shape
+    inner = conv_inner.shape[1]
     state = w_group.shape[3]
     heads = w_step.shape[1]
-    local = lax.axis_index("col") * w_group.shape[2] // lax.axis_size("col")
-
-    def pick_group(table, axis):
-        return lax.dynamic_index_in_dim(table, local, axis, keepdims=False)
-
-    taps = jnp.concatenate(
-        [conv_inner, jnp.reshape(pick_group(conv_group, 2), (kernel, 2 * state))], axis=1
-    )
-    bias = jnp.concatenate(
-        [conv_bias_inner, jnp.reshape(pick_group(conv_bias_group, 1), (2 * state,))]
-    )[None, :]
-    edges = jnp.concatenate(
-        [
-            jnp.transpose(edge_inner, (1, 0, 2)),
-            jnp.transpose(
-                jnp.reshape(pick_group(edge_group, 3), (requests, kernel - 1, 2 * state)), (1, 0, 2)
-            ),
-        ],
-        axis=2,
-    )
-    edges = jnp.reshape(edges, ((kernel - 1) * requests, inner + 2 * state))
     gate_in, chan, step_raw, rim = project(tokens, w_inner, w_group, w_step, pre_gain)
     arrays = scan(
-        lengths, deal, step_bias, decay_log, skip, chan, rim, step_raw, taps, bias, edges, init_states
+        lengths,
+        deal,
+        step_bias,
+        decay_log,
+        skip,
+        chan,
+        rim,
+        step_raw,
+        conv_inner,
+        conv_group,
+        conv_bias_inner,
+        conv_bias_group,
+        edge_inner,
+        edge_group,
+        init_states,
     )
     hidden_out, final_states, logits = finish(
         lengths, deal, arrays, gate_in, inner_gain, w_out, tokens, w_head, final_gain
     )
+    hidden_out, final_states, logits = deliver(hidden_out, final_states, logits)
     final_states = jnp.reshape(
         final_states, (final_states.shape[0], heads, inner // heads, state)
     )

time: 117 us -> 102 us (0.87)
  local copies, waits for them, and re-layouts: 7 us -> 0 us
  Pallas kernels: 105 us -> 101 us
  other arithmetic: 3.42 us -> 0 us
    pallas_call x1, Pallas kernels: 55.3 us -> 48.8 us  [finish(): pl.pallas_call(finish_kernel, out_shape=[jax.ShapeDtypeStruct((rows, feat...]
    unnamed x6 -> x0, local copies, waits for them, and re-layouts: 4.89 us -> none
    concatenate x3 -> x0, other arithmetic: 3.42 us -> none  [the longest x1 1.44 us: per_device(): jnp.concatenate([jnp.transpose(edge_inner, (1, 0, 2)), jnp.transpose(jnp....]
    pallas_call x0 -> x1, Pallas kernels: none -> 2.02 us  [deliver(): pl.pallas_call(deliver_kernel, out_shape=[jax.ShapeDtypeStruct(a.shape, a...]
    dynamic_slice x4 -> x0, local copies, waits for them, and re-layouts: 1.48 us -> none  [pick_group(): return lax.dynamic_index_in_dim(table, local, axis, keepdims=False)]
where the time goes in v1:
time: 102 us
  Pallas kernels  101 us (99%)
    pallas_call x1, Pallas kernels, finish(): pl.pallas_call(finish_kernel, out_shape=[jax.ShapeDtypeStruct((rows, feat...  48.8 us
    pallas_call x1, Pallas kernels, project(): pl.pallas_call(project_kernel, out_shape=[jax.ShapeDtypeStruct((rows, wid...  39.7 us
    pallas_call x1, Pallas kernels, scan(): pl.pallas_call(scan_kernel, out_shape=[shape((rows, inner), f32), shape((...  10.6 us

profile of v1, /device:TPU:0, one launch (start us, length us, event | category | flops | bytes accessed | tf_op | source)
XLA Modules:
  0.0 101.9 jit_solution(13290052635463570204)
XLA Ops:
  0.6 39.7 %project.1 = (bf16[512,512]{1,0:T(8,128)(2,1)}, bf16[512,768]{1,0:T(8,128)(2,1)}, f32[512,8]{1,0:T(8,128)}, bf16[16,768]{1,0:T(8,128)(2,1)}) custom-call(bf16[512,256]{1,0:T(8,128)(2,1)} %tokens.3, bf16[4096,2,512]{2,1,0:T(2,128)(2,1)} %w_inner.1, bf16[4096,2,2,128]{3,2,1,0:T(2,128)(2,1)} %w_group.1, bf16[8,4096]{1,0:T(8,128)(2,1)} %bitcast.9, ...), custom_call_target="tpu_custom_call" | custom-call | tf_op jit(solution)/shard_map/project/pallas_call | solution.py:264
  40.3 10.6 %scan.1 = (f32[512,512]{1,0:T(8,128)}, bf16[512,768]{1,0:T(8,128)(2,1)}, f32[512,128]{1,0:T(8,128)}, f32[8,512]{1,0:T(8,128)}, f32[8,512]{1,0:T(8,128)}, /*index...) custom-call(s32[16]{0:T(128)} %lengths.3, ...), custom_call_target="tpu_custom_call" | custom-call | tf_op jit(solution)/shard_map/scan/pallas_call | solution.py:560
  50.9 48.8 %finish.1 = (bf16[512,256]{1,0:T(8,128)(2,1)}, f32[2,512,128]{2,1,0:T(8,128)}, f32[16,256]{1,0:T(8,128)}) custom-call(s32[16]{0:T(128)} %lengths.3, s32[16]{0:T(128)} %deal.3, f32[512,512]{1,0:T(8,128)} %get-tuple-element.27.partial_y, bf16[512,768]{1,0:T(8,128)(2,1)} %get-tuple-element.28.mixed, f32[512,128]{1,0:T(8,128)} %get-tuple-element.29.decay_column, ...), custom_call_target="tpu_custom_call" | custom-call | tf_op jit(solution)/shard_map/finish/pallas_call | solution.py:1008
  99.7 2.0 %deliver.1 = (bf16[512,256]{1,0:T(8,128)(2,1)}, f32[2,512,128]{2,1,0:T(8,128)}, f32[16,256]{1,0:T(8,128)}) custom-call(bf16[512,256]{1,0:T(8,128)(2,1)} %get-tuple-element.39.refs_0_, f32[2,512,128]{2,1,0:T(8,128)} %get-tuple-element.40.refs_1_, f32[16,256]{1,0:T(8,128)} %get-tuple-element.41.refs_2_), custom_call_target="tpu_custom_call" | custom-call | tf_op jit(solution)/shard_map/deliver/pallas_call | solution.py:1088

commit v2 on v1

--- a/solution.py
+++ b/solution.py
@@ -173,28 +173,34 @@
     total_step[...] = jnp.zeros_like(total_step)
     squares[...] = jnp.zeros_like(squares)
 
-    def multiply(half, du, dv):
-        block = block_of(half, du, dv)
+    def multiply(half, places):
         rows = pl.ds(pl.multiple_of(half * HALF, HALF), HALF)
-        column = pl.multiple_of(block * FEAT, FEAT)
-        wide = held[block, rows, :].astype(jnp.float32)
-        squares[rows, :] += wide[:, :lanes] * wide[:, :lanes] + wide[:, lanes:] * wide[:, lanes:]
-        scaled = (wide * gain[:, pl.ds(column, FEAT)]).astype(jnp.bfloat16)
-        total[rows, :] += jnp.dot(
-            scaled, weights[pl.ds(column, FEAT), :], preferred_element_type=jnp.float32
-        )
-        total_step[rows, :] += lax.dot_general(
-            scaled,
-            w_step[:, pl.ds(column, FEAT)],
-            (((1,), (1,)), ((), ())),
-            preferred_element_type=jnp.float32,
-        )
+        value = 0.0
+        step_value = 0.0
+        square = 0.0
+        for du, dv in places:
+            block = block_of(half, du, dv)
+            column = pl.multiple_of(block * FEAT, FEAT)
+            wide = held[block, rows, :].astype(jnp.float32)
+            square = square + wide[:, :lanes] * wide[:, :lanes]
+            square = square + wide[:, lanes:] * wide[:, lanes:]
+            scaled = (wide * gain[:, pl.ds(column, FEAT)]).astype(jnp.bfloat16)
+            value = value + jnp.dot(
+                scaled, weights[pl.ds(column, FEAT), :], preferred_element_type=jnp.float32
+            )
+            step_value = step_value + lax.dot_general(
+                scaled,
+                w_step[:, pl.ds(column, FEAT)],
+                (((1,), (1,)), ((), ())),
+                preferred_element_type=jnp.float32,
+            )
+        squares[rows, :] += square
+        total[rows, :] += value
+        total_step[rows, :] += step_value
 
     def run(count, pick):
         def body(i, carry):
-            half = lax.rem(i, 2)
-            du, dv = pick(i // 2)
-            multiply(half, du, dv)
+            multiply(lax.rem(i, 2), pick(i // 2))
             return carry
 
         lax.fori_loop(0, 2 * count, body, 0)
@@ -216,20 +222,20 @@
         spread(half, 3)
     untangle(3)
     own_copy.wait()
-    run(2, lambda j: (j, 0))
+    run(1, lambda j: ((0, 0), (1, 0)))
     for half in (0, 1):
         relay(half, 1)
-    run(2, lambda j: (j + 2, 0))
+    run(1, lambda j: ((2, 0), (-1, 0)))
     for half in (0, 1):
         relay(half, 2)
-    run(4, lambda j: (-(j // 2), 2 * lax.rem(j, 2) - 1))
+    run(1, lambda j: ((0, -1), (0, 1), (-1, -1), (-1, 1)))
     for half in (0, 1):
         relay(half, 3)
-    run(4, lambda j: (1 + j // 2, 2 * lax.rem(j, 2) - 1))
-    for k in range(4):
+    run(1, lambda j: ((1, -1), (1, 1), (2, -1), (2, 1)))
+    for k in (0, 2):
         for half in (0, 1):
-            arrive(half, 6 + 4 * k, 7 + 4 * k)
-        run(1, lambda j: (ORDER[k], 2))
+            arrive(half, 6 + 4 * k, 7 + 4 * k, 10 + 4 * k, 11 + 4 * k)
+        run(1, lambda j: ((ORDER[k], 2), (ORDER[k + 1], 2)))
     for half in (0, 1):
         for number in range(20):
             messages[half, number].wait_send()
@@ -872,13 +878,6 @@
     chip = lax.axis_index("seq") // 2
     chips = seq // 2
 
-    def fill(o, carry):
-        value = finals_own[o].astype(jnp.float32) + by_head(factor_own[o], size) * entry_held[...]
-        outbox[lax.rem(o // 2, 2), o // 4, lax.rem(o, 2)] = value.astype(jnp.bfloat16)
-        return carry
-
-    lax.fori_loop(0, requests, fill, 0)
-    pair_copy = hand(outbox.at[1 - core], pair_land, 4, {"seq": spot("seq", 1 - 2 * core)})
     for k in range(4):
         for half in (0, 1):
             for side in (0, 1):
@@ -893,6 +892,13 @@
                     8 + 2 * k,
                     AXES[half][1],
                 )
+    def fill(o, carry):
+        value = finals_own[o].astype(jnp.float32) + by_head(factor_own[o], size) * entry_held[...]
+        outbox[lax.rem(o // 2, 2), o // 4, lax.rem(o, 2)] = value.astype(jnp.bfloat16)
+        return carry
+
+    lax.fori_loop(0, requests, fill, 0)
+    pair_copy = hand(outbox.at[1 - core], pair_land, 4, {"seq": spot("seq", 1 - 2 * core)})
     row_total = partials[0, 15, HALF:PITCH]
     row_total = row_total + jnp.dot(chooser, tokens[...], preferred_element_type=jnp.float32)
     for j, copy in enumerate(row_copies):

time: 102 us -> 100 us (0.980)
  Pallas kernels: 101 us -> 98.9 us
    pallas_call x1, Pallas kernels: 39.7 us -> 36.3 us  [project(): pl.pallas_call(project_kernel, out_shape=[jax.ShapeDtypeStruct((rows, wid...]
    pallas_call x1, Pallas kernels: 48.8 us -> 51.4 us  [finish(): pl.pallas_call(finish_kernel, out_shape=[jax.ShapeDtypeStruct((rows, feat...]
    pallas_call x1, Pallas kernels: 10.6 us -> 9.19 us  [scan(): pl.pallas_call(scan_kernel, out_shape=[shape((rows, inner), f32), shape((...]
where the time goes in v2:
time: 100 us; the launch traced here: 99.7 us
  Pallas kernels  98.9 us (99%)
    pallas_call x1, Pallas kernels, finish(): pl.pallas_call(finish_kernel, out_shape=[jax.ShapeDtypeStruct((rows, feat...  51.4 us
    pallas_call x1, Pallas kernels, project(): pl.pallas_call(project_kernel, out_shape=[jax.ShapeDtypeStruct((rows, wid...  36.3 us
    pallas_call x1, Pallas kernels, scan(): pl.pallas_call(scan_kernel, out_shape=[shape((rows, inner), f32), shape((...  9.19 us
    pallas_call x1, Pallas kernels, deliver(): pl.pallas_call(deliver_kernel, out_shape=[jax.ShapeDtypeStruct(a.shape, a...  2.02 us

profile of v2, /device:TPU:0, one launch (start us, length us, event | category | flops | bytes accessed | tf_op | source)
XLA Modules:
  0.0 99.7 jit_solution(17643331000962839355)
XLA Ops:
  0.6 36.3 %project.1 = (bf16[512,512]{1,0:T(8,128)(2,1)}, bf16[512,768]{1,0:T(8,128)(2,1)}, f32[512,8]{1,0:T(8,128)}, bf16[16,768]{1,0:T(8,128)(2,1)}) custom-call(bf16[512,256]{1,0:T(8,128)(2,1)} %tokens.3, bf16[4096,2,512]{2,1,0:T(2,128)(2,1)} %w_inner.1, bf16[4096,2,2,128]{3,2,1,0:T(2,128)(2,1)} %w_group.1, bf16[8,4096]{1,0:T(8,128)(2,1)} %bitcast.9, ...), custom_call_target="tpu_custom_call" | custom-call | tf_op jit(solution)/shard_map/project/pallas_call | solution.py:270
  36.9 9.2 %scan.1 = (f32[512,512]{1,0:T(8,128)}, bf16[512,768]{1,0:T(8,128)(2,1)}, f32[512,128]{1,0:T(8,128)}, f32[8,512]{1,0:T(8,128)}, f32[8,512]{1,0:T(8,128)}, /*index...) custom-call(s32[16]{0:T(128)} %lengths.3, ...), custom_call_target="tpu_custom_call" | custom-call | tf_op jit(solution)/shard_map/scan/pallas_call | solution.py:566
  46.1 51.4 %finish.1 = (bf16[512,256]{1,0:T(8,128)(2,1)}, f32[2,512,128]{2,1,0:T(8,128)}, f32[16,256]{1,0:T(8,128)}) custom-call(s32[16]{0:T(128)} %lengths.3, s32[16]{0:T(128)} %deal.3, f32[512,512]{1,0:T(8,128)} %get-tuple-element.27.partial_y, bf16[512,768]{1,0:T(8,128)(2,1)} %get-tuple-element.28.mixed, f32[512,128]{1,0:T(8,128)} %get-tuple-element.29.decay_column, ...), custom_call_target="tpu_custom_call" | custom-call | tf_op jit(solution)/shard_map/finish/pallas_call | solution.py:1014
  97.5 2.0 %deliver.1 = (bf16[512,256]{1,0:T(8,128)(2,1)}, f32[2,512,128]{2,1,0:T(8,128)}, f32[16,256]{1,0:T(8,128)}) custom-call(bf16[512,256]{1,0:T(8,128)(2,1)} %get-tuple-element.39.refs_0_, f32[2,512,128]{2,1,0:T(8,128)} %get-tuple-element.40.refs_1_, f32[16,256]{1,0:T(8,128)} %get-tuple-element.41.refs_2_), custom_call_target="tpu_custom_call" | custom-call | tf_op jit(solution)/shard_map/deliver/pallas_call | solution.py:1094
